TPU v7x, 32 devices: a whole 2x2x4 slice. The times are simulated.
32 devices in a mesh: grp: 4 (over x, core), row: 8 (over z, y).
Axes of the slice: x: 2, y: 2, z: 4, core: 2. Of those that a mesh axis runs over, the one named last changes fastest.
Arguments:
- table: float32 [8, 65536, 128], P('grp', 'row'), may hold values from -6 to 6
- row_shard: int32 [8, 8192, 1], P('grp'), may hold values from 0 to 7; in each aligned block of 256 rows (0 to 255, 256 to 511, ..., all dimensions but the last counted through in order) at most 96 rows name the same one
- row_offset: int32 [8, 8192], P('grp'), may hold values from 0 to 8191
- bag_lengths: int32 [8, 32, 128], P('grp'), may hold values from 1 to 4, 256 in all within a row
Outputs:
- pooled: float32 [8, 4096, 128], P(None, ('grp', 'row'))
Inputs may be any that keep to these rules, and one draw needn't show every extreme that they name: `row_shard`: in each aligned block of 256 lookups of a table (the lookups of one block of bags), at most 96 lookups name the same row shard, and in every draw some block reaches 96. `bag_lengths`: the 128 lengths of each block sum to 256.
All inputs are finite; a program needn't handle non-finite values.
Results may differ from a plain program's by a relative error of at most 0.0003.
Values sent between devices are 32-bit elements; how exact they have to be, the bound alone decides.
A program may use at most 64 MiB of HBM per device.

v0:
```python
import jax
import jax.numpy as jnp
from jax import lax
from jax.sharding import PartitionSpec as P


def fetch_rows(table, index):
    flat = index.reshape(index.shape[0], -1)
    picked = jax.vmap(lambda matrix, wanted: jnp.take(matrix, wanted, axis=0))(table, flat)
    return picked.reshape(index.shape + (table.shape[-1],))


def body(table, row_shard, row_offset, bag_lengths):
    groups = lax.axis_size("grp")
    shards = lax.axis_size("row")
    mine = lax.axis_index("row")
    tables_here = table.shape[0]
    width = table.shape[2]
    bags_block = bag_lengths.shape[2]
    look_block = row_offset.shape[1] // (groups * shards)
    capacity = 3 * look_block // shards
    owner = row_shard.reshape(tables_here, groups, shards, look_block)
    offset = row_offset.reshape(tables_here, groups, shards, look_block)
    lengths = bag_lengths.reshape(tables_here, groups, shards, bags_block)
    local = (owner == mine).astype(jnp.int32)
    rank = jnp.cumsum(local, axis=3) - local
    ends = jnp.cumsum(lengths, axis=-1)
    places = lax.broadcasted_iota(jnp.int32, (look_block, bags_block), 0)
    within = jnp.sum((ends[..., None, :] <= places).astype(jnp.int32), axis=-1)
    slots = lax.broadcasted_iota(jnp.int32, (capacity,), 0)
    match = (local[..., None] == 1) & (rank[..., None] == slots)
    packed_offset = jnp.sum(jnp.where(match, offset[..., None], 0), axis=3)
    packed_bag = jnp.sum(jnp.where(match, within[..., None] + 1, 0), axis=3) - 1
    vectors = fetch_rows(table, packed_offset)
    vectors = vectors.reshape(tables_here, groups * shards, capacity, width)
    packed_bag = packed_bag.reshape(tables_here, groups * shards, capacity)
    got_rows, got_bags = (
        lax.all_to_all(vectors, ("grp", "row"), split_axis=1, concat_axis=1, tiled=True),
        lax.all_to_all(packed_bag, ("grp", "row"), split_axis=1, concat_axis=1, tiled=True),
    )
    bag_ids = lax.broadcasted_iota(jnp.int32, (bags_block, capacity), 0)
    weights = (got_bags[:, :, None, :] == bag_ids).astype(jnp.float32)
    weights = weights.reshape(tables_here, groups, shards, bags_block, capacity)
    got_rows = got_rows.reshape(tables_here, groups, shards, capacity, width)
    pooled = jnp.einsum("tgsbc,tgsce->gtbe", weights, got_rows, precision=lax.Precision.HIGHEST)
    return pooled.reshape(groups * tables_here, bags_block, width)


def solution(mesh):
    placed = (P("grp", "row", None), P("grp", None, None), P("grp", None), P("grp", None, None))
    return jax.shard_map(
        body, mesh=mesh, in_specs=placed, out_specs=P(None, ("grp", "row"), None), check_vma=False
    )
```

profile of v0, /device:TPU:24, one launch (start us, length us, event | category | flops | bytes accessed | tf_op | source)
XLA Modules:
  0.0 332.8 jit_solution(793737041661239388)
XLA Ops:
  0.0 4.1 %reduce_window_sum.35 = s32[2,4,8,128]{3,2,1,0:T(8,128)S(1)} reduce-window(s32[2,4,8,128]{3,2,1,0:T(8,128)} %bitcast.45, s32[]{:T(128)} %constant.27.clone.1), window={size=1x1x1x128 pad=0_0x0_0x0_0x127_0}, to_apply=%region_2.3 | reduce-window | flops 1040384 | bytes 65540 | tf_op jit(solution)/shard_map/jit(cumsum)/reduce_window_sum | solution.py:27
  4.1 2.2 convert_reduce_fusion
  6.4 0.8 copy.56
  7.2 1.1 fusion.10
  8.3 4.5 %reduce-window.6 = s32[2,4,8,2,128]{4,2,3,1,0:T(8,128)S(1)} reduce-window(s32[2,4,8,2,128]{4,2,3,1,0:T(8,128)S(1)} %copy.32, s32[]{:T(128)} %constant.27.clone.1), window={size=1x1x1x1x128 pad=0_0x0_0x0_0x0_0x127_0}, to_apply=%region_0.0 | reduce-window | flops 2080768 | bytes 131076 | tf_op jit(solution)/shard_map/reduce-window
  12.9 0.1 slice.10
  12.9 0.2 copy.33
  13.1 0.1 bitcast_subtract_fusion
  13.2 2.8 select_reduce_fusion.1
  16.0 0.6 copy.35
  16.7 5.9 %all-to-all-start = ((s32[2,32,96]{2,0,1:T(2,128)}), s32[2,32,96]{2,0,1:T(2,128)S(1)}, u32[]{:S(2)}, u32[]{:S(2)}) async-start(s32[2,32,96]{2,0,1:T(2,128)} %copy.35), calls=%async_computation | async-start | bytes 65536 | tf_op jit(solution)/shard_map/all_to_all | solution.py:39
  22.6 0.1 reshape.108
  22.7 223.6 %gather_fusion = f32[6144,128]{1,0:T(8,128)S(1)} fusion(f32[2,8192,128]{2,1,0:T(8,128)} %param.4, s32[6144]{0:T(1024)S(1)} %bitcast.36), kind=kCustom, calls=%fused_computation | custom fusion | bytes 6340608 | tf_op jit(solution)/shard_map/vmap(jit(_take))/gather | solution.py:9
  246.3 2.6 copy_select_fusion
  249.0 0.0 all-to-all-done
  249.0 8.4 %all-to-all-start.1 = ((f32[2,32,96,128]{3,2,0,1:T(8,128)}), f32[2,32,96,128]{3,2,0,1:T(8,128)S(1)}, u32[]{:S(2)}, u32[]{:S(2)}) async-start(f32[2,32,96,128]{3,2,0,1:T(8,128)} %copy_select_fusion), calls=%async_computation.1 | async-start | bytes 6291456 | tf_op jit(solution)/shard_map/all_to_all | solution.py:38
  257.3 70.5 %all-to-all-done.1 = f32[2,32,96,128]{3,2,0,1:T(8,128)S(1)} async-done(((f32[2,32,96,128]{3,2,0,1:T(8,128)}), f32[2,32,96,128]{3,2,0,1:T(8,128)S(1)}, u32[]{:S(2)}, u32[]{:S(2)}) %all-to-all-start.1) | async-done | bytes 3145760 | tf_op jit(solution)/shard_map/all_to_all | solution.py:38
  327.9 4.9 %fusion.1 = f32[4,2,128,128,1]{3,2,4,1,0:T(8,128)} fusion(f32[2,4,8,96,128]{4,3,0,2,1:T(8,128)S(1)} %bitcast.37, s32[2,4,8,96]{3,2,0,1:T(8,128)S(1)} %copy.37), kind=kOutput, calls=%fused_computation.7 | convolution fusion | flops 1208745984 | bytes 3694592 | tf_op jit(solution)/shard_map/tgsbc,tgsce->gtbe/dot_general | solution.py:45
  (11 shorter events, 0.1 us)
Async XLA Ops:
  16.7 232.3 %all-to-all-start = ((s32[2,32,96]{2,0,1:T(2,128)}), s32[2,32,96]{2,0,1:T(2,128)S(1)}, u32[]{:S(2)}, u32[]{:S(2)}) async-start(s32[2,32,96]{2,0,1:T(2,128)} %copy.35), calls=%async_computation | async-start | bytes 65536 | tf_op jit(solution)/shard_map/all_to_all | solution.py:39
  249.0 78.9 %all-to-all-start.1 = ((f32[2,32,96,128]{3,2,0,1:T(8,128)}), f32[2,32,96,128]{3,2,0,1:T(8,128)S(1)}, u32[]{:S(2)}, u32[]{:S(2)}) async-start(f32[2,32,96,128]{3,2,0,1:T(8,128)} %copy_select_fusion), calls=%async_computation.1 | async-start | bytes 6291456 | tf_op jit(solution)/shard_map/all_to_all | solution.py:38
where the time goes:
time: 338 us; the launch traced here: 333 us
  local copies, waits for them, and re-layouts  225 us (67%)
  waiting for transfers between devices  70.5 us (21%)
  other arithmetic  17.5 us (5%)
  starting transfers between devices  14.2 us (4%)
  matrix products  4.91 us (1%)
    gather x1, local copies, waits for them, and re-layouts, fetch_rows(): jnp.take(matrix, wanted, axis=0)  224 us
    all_to_all x1, waiting for transfers between devices, body(): lax.all_to_all(vectors, ('grp', 'row'), split_axis=1, concat_axis=1, tile...  70.5 us
    all_to_all x1, starting transfers between devices, body(): lax.all_to_all(vectors, ('grp', 'row'), split_axis=1, concat_axis=1, tile...  8.36 us
  transfers between devices with their start and end apart: 2, of which 1 were waited for; matrix products, arithmetic and copies ran while one was open for 68% of the time, Pallas kernels for 0%

commit v1 on v0

v1 whole, which is shorter than its diff:
```python
import functools
import jax
import jax.numpy as jnp
from jax import lax
from jax.experimental import pallas as pl
from jax.experimental.pallas import tpu as pltpu
from jax.sharding import PartitionSpec as P

MESH = pl.DeviceIdType.MESH


def kernel(dims, off_ref, bag_ref, table_hbm, out_ref, *scratch):
    tables, groups, shards, cap, bags = dims
    held = scratch[:tables]
    (ysend, comb, part, fromleft, fromright,
     tab_sem, ys_sem, yr_sem, zs_sem, lr_sem, rr_sem, fs_sem, fr_sem, own_sem) = scratch[tables:]
    line = shards // 2
    g = lax.axis_index("grp")
    r = lax.axis_index("row")
    q = r // 2
    p = r % 2
    mate = q * 2 + 1 - p

    loads = [pltpu.make_async_copy(table_hbm.at[t], held[t], tab_sem.at[t]) for t in range(tables)]
    for load in loads:
        load.start()

    barrier = pltpu.get_barrier_semaphore()
    pl.semaphore_signal(barrier, inc=1, device_id=(g, mate), device_id_type=MESH)

    @pl.when(q > 0)
    def _():
        pl.semaphore_signal(barrier, inc=1, device_id=(g, r - 2), device_id_type=MESH)

    @pl.when(q < line - 1)
    def _():
        pl.semaphore_signal(barrier, inc=1, device_id=(g, r + 2), device_id_type=MESH)

    for step in range(1, groups):
        pl.semaphore_signal(barrier, inc=1, device_id=((g + step) % groups, r), device_id_type=MESH)
    pl.semaphore_wait(barrier, groups + jnp.where(q > 0, 1, 0) + jnp.where(q < line - 1, 1, 0))

    def target(j):
        picked = 0
        for at in range(line):
            order = sorted(range(line), key=lambda d: (-abs(d - at), d))
            picked = picked + jnp.where(q == at, order[j], 0)
        return picked

    def ycopy(c):
        return pltpu.make_async_remote_copy(
            src_ref=ysend.at[c], dst_ref=comb.at[c, :, 1], send_sem=ys_sem.at[c], recv_sem=yr_sem.at[c],
            device_id=(g, mate), device_id_type=MESH)

    def rightcopy(c):
        return pltpu.make_async_remote_copy(
            src_ref=part.at[c], dst_ref=fromleft.at[c], send_sem=zs_sem.at[c], recv_sem=lr_sem.at[c],
            device_id=(g, r + 2), device_id_type=MESH)

    def leftcopy(c):
        return pltpu.make_async_remote_copy(
            src_ref=part.at[c], dst_ref=fromright.at[c], send_sem=zs_sem.at[c], recv_sem=rr_sem.at[c],
            device_id=(g, r - 2), device_id_type=MESH)

    def fcopy(c, t, step, towards):
        other = (g + towards * step + groups) % groups
        slot = t * groups + step
        return pltpu.make_async_remote_copy(
            src_ref=part.at[c, other], dst_ref=out_ref.at[g * tables + t], send_sem=fs_sem.at[slot],
            recv_sem=fr_sem.at[slot], device_id=(other, r), device_id_type=MESH)

    def gather(table, dst, base):
        @pl.loop(0, cap // 8)
        def _(i):
            for u in range(8):
                row = off_ref[base + i * 8 + u]
                dst[pl.ds(i * 8 + u, 1), :] = table[pl.ds(row, 1), :]

    def block(t, k, to, side):
        return ((t * groups + k) * line + to) * 2 + side

    def fetch(j, t):
        to = target(j)
        c = to * tables + t

        @pl.loop(0, groups)
        def _(k):
            gather(held[t], ysend.at[c, k], block(t, k, to, 1 - p) * cap)
        ycopy(c).start()

        @pl.loop(0, groups)
        def _(k):
            gather(held[t], comb.at[c, k, 0], block(t, k, to, p) * cap)

    def merge(j, t):
        to = target(j)
        c = to * tables + t
        ycopy(c).wait_recv()
        places = lax.broadcasted_iota(jnp.int32, (bags, 2 * cap), 0)

        @pl.loop(0, groups)
        def _(k):
            spot = (t * groups + k) * line + to
            weights = jnp.where(places == bag_ref[pl.ds(spot, 1), :], 1.0, 0.0).astype(jnp.bfloat16)
            vectors = jnp.concatenate([comb[c, k, 0], comb[c, k, 1]], axis=0)
            high = vectors.astype(jnp.bfloat16)
            low = (vectors - high.astype(jnp.float32)).astype(jnp.bfloat16)
            part[c, k] = (jnp.dot(weights, high, preferred_element_type=jnp.float32)
                          + jnp.dot(weights, low, preferred_element_type=jnp.float32))

        def add(buffer):
            @pl.loop(0, groups)
            def _(k):
                part[c, k] = part[c, k] + buffer[c, k]

        @pl.when(jnp.logical_and(to >= q, q > 0))
        def _():
            rightcopy(c).wait_recv()
            add(fromleft)

        @pl.when(jnp.logical_and(to <= q, q < line - 1))
        def _():
            leftcopy(c).wait_recv()
            add(fromright)

        if j < line - 1:
            @pl.when(to > q)
            def _():
                rightcopy(c).start()

            @pl.when(to < q)
            def _():
                leftcopy(c).start()
        else:
            for step in range(1, groups):
                fcopy(c, t, step, 1).start()
            pltpu.make_async_copy(part.at[c, g], out_ref.at[g * tables + t], own_sem.at[t]).start()

    items = [(j, t) for j in range(line) for t in range(tables)]
    for n, (j, t) in enumerate(items):
        if n < tables:
            loads[t].wait()
        fetch(j, t)
        if n > 0:
            merge(*items[n - 1])
    merge(*items[-1])

    for j, t in items:
        to = target(j)
        c = to * tables + t
        ycopy(c).wait_send()
        if j < line - 1:
            rightcopy(c).wait_send()
    for t in range(tables):
        c = q * tables + t
        pltpu.make_async_copy(part.at[c, g], out_ref.at[g * tables + t], own_sem.at[t]).wait()
        for step in range(1, groups):
            fcopy(c, t, step, 1).wait_send()
            origin = (g - step + groups) % groups
            slot = t * groups + step
            pltpu.make_async_remote_copy(
                src_ref=part.at[c, g], dst_ref=out_ref.at[origin * tables + t], send_sem=fs_sem.at[slot],
                recv_sem=fr_sem.at[slot], device_id=(origin, r), device_id_type=MESH).wait_recv()


def body(table, row_shard, row_offset, bag_lengths):
    groups = lax.axis_size("grp")
    shards = lax.axis_size("row")
    line = shards // 2
    mine = lax.axis_index("row")
    side = mine % 2
    tables, rows, width = table.shape
    bags = bag_lengths.shape[2]
    look = row_offset.shape[1] // (groups * shards)
    cap = 3 * look // shards
    blocks = groups * shards
    owner = row_shard.reshape(tables * blocks, look)
    offset = row_offset.reshape(tables * blocks, look)
    before = jnp.triu(jnp.ones((look, look), jnp.bfloat16), 1)

    def ranks(owners, shard):
        local = owners == shard
        rank = jnp.dot(local.astype(jnp.bfloat16), before, preferred_element_type=jnp.float32).astype(jnp.int32)
        return jnp.where(local, rank, -1)

    def pack(rank, values):
        slots = lax.broadcasted_iota(jnp.int32, (1, cap, 1), 1)
        return jnp.sum(jnp.where(rank[:, None, :] == slots, values[:, None, :], 0), axis=2)

    packed_offset = pack(ranks(owner, mine), offset)
    near = lax.dynamic_index_in_dim(owner.reshape(tables * groups * line, 2, look), side, 1, keepdims=False)
    lengths = lax.dynamic_index_in_dim(bag_lengths.reshape(tables * groups * line, 2, bags), side, 1, keepdims=False)
    upto = jnp.triu(jnp.ones((bags, bags), jnp.bfloat16))
    ends = jnp.dot(lengths.astype(jnp.bfloat16), upto, preferred_element_type=jnp.float32).astype(jnp.int32)
    places = lax.broadcasted_iota(jnp.int32, (1, 1, look), 2)
    within = jnp.sum((ends[:, :, None] <= places).astype(jnp.int32), axis=1)
    mate = mine + 1 - 2 * side
    packed_bag = jnp.concatenate([pack(ranks(near, mine), within + 1), pack(ranks(near, mate), within + 1)], axis=1) - 1

    chunks = line * tables
    dims = (tables, groups, shards, cap, bags)
    return pl.pallas_call(
        functools.partial(kernel, dims),
        out_shape=jax.ShapeDtypeStruct((groups * tables, bags, width), jnp.float32),
        in_specs=[pl.BlockSpec(memory_space=pltpu.SMEM), pl.BlockSpec(memory_space=pltpu.VMEM), pl.BlockSpec(memory_space=pl.ANY)],
        out_specs=pl.BlockSpec(memory_space=pltpu.VMEM),
        scratch_shapes=[
            *[pltpu.VMEM((rows, width), jnp.float32) for _ in range(tables)],
            pltpu.VMEM((chunks, groups, cap, width), jnp.float32),
            pltpu.VMEM((chunks, groups, 2, cap, width), jnp.float32),
            pltpu.VMEM((chunks, groups, bags, width), jnp.float32),
            pltpu.VMEM((chunks, groups, bags, width), jnp.float32),
            pltpu.VMEM((chunks, groups, bags, width), jnp.float32),
            pltpu.SemaphoreType.DMA((tables,)),
            pltpu.SemaphoreType.DMA((chunks,)),
            pltpu.SemaphoreType.DMA((chunks,)),
            pltpu.SemaphoreType.DMA((chunks,)),
            pltpu.SemaphoreType.DMA((chunks,)),
            pltpu.SemaphoreType.DMA((chunks,)),
            pltpu.SemaphoreType.DMA((tables * groups,)),
            pltpu.SemaphoreType.DMA((tables * groups,)),
            pltpu.SemaphoreType.DMA((tables,)),
        ],
        compiler_params=pltpu.CompilerParams(collective_id=0, has_side_effects=True, vmem_limit_bytes=63 * 2**20),
    )(packed_offset.reshape(-1), packed_bag, table)


def solution(mesh):
    placed = (P("grp", "row", None), P("grp", None, None), P("grp", None), P("grp", None, None))
    return jax.shard_map(
        body, mesh=mesh, in_specs=placed, out_specs=P(None, ("grp", "row"), None), check_vma=False
    )
```

time: 338 us -> 68.2 us (0.20)
  the two profiles are of different devices: /device:TPU:24 before, /device:TPU:17 now
where the time goes in v1:
time: 68.2 us; the launch traced here: 67.7 us
  Pallas kernels  56.6 us (83%)
  other arithmetic  6.75 us (10%)
  local copies, waits for them, and re-layouts  3.62 us (5%)
    pallas_call x1, Pallas kernels, body(): pl.pallas_call(functools.partial(kernel, dims), out_shape=jax.ShapeDtypeS...  56.6 us
    reduce_sum x2, other arithmetic, pack(): jnp.sum(jnp.where(rank[:, None, :] == slots, values[:, None, :], 0), axis=2)  2.47 us
    unnamed x1, local copies, waits for them, and re-layouts  1.87 us

profile of v1, /device:TPU:17, one launch (start us, length us, event | category | flops | bytes accessed | tf_op | source)
XLA Modules:
  0.0 67.7 jit_solution(4832488883930175298)
XLA Ops:
  0.0 0.8 %dynamic-slice_convert_fusion = bf16[32,1,128]{2,1,0:T(2,128)(2,1)S(1)} fusion(s32[32,2,128]{2,1,0:T(2,128)} %bitcast.11, s32[]{:T(128)S(6)} %select_n.51), kind=kLoop, calls=%fused_computation.38 | loop fusion | flops 4096 | bytes 24580 | tf_op jit(solution)/shard_map/convert_element_type | solution.py:194
  0.8 0.2 convolution_convert_fusion.3
  1.0 0.7 %convert_reduce_fusion = s32[32,256]{1,0:T(8,128)S(1)} fusion(s32[32,128]{1,0:T(8,128)S(1)} %convolution_convert_fusion.3), kind=kLoop, calls=%fused_computation.2 | loop fusion | flops 3137536 | bytes 49152 | tf_op jit(solution)/shard_map/reduce_sum | solution.py:196
  1.7 1.1 %compare_reduce_fusion = pred[2,8192]{1,0:T(4,128)(4,1)S(1)} fusion(s32[2,8192,1]{1,2,0:T(1,128)} %param.5, s32[]{:T(128)S(6)} %axis_index.12), kind=kLoop, calls=%fused_computation.17 | loop fusion | flops 16384 | bytes 81924 | tf_op jit(solution)/shard_map/eq | solution.py:182
  2.8 0.1 eq.70
  2.8 0.2 fusion
  3.0 0.9 %broadcast_in_dim.62 = s32[64,256]{1,0:T(8,128)S(1)} reshape(s32[2,8192]{1,0:T(2,128)} %param.6) | data formatting | bytes 131072 | tf_op jit(solution)/shard_map/jit(_where)/broadcast_in_dim | solution.py:188
  3.9 1.3 %select_reduce_fusion = s32[64,96]{1,0:T(8,128)S(1)} fusion(s32[64,256]{1,0:T(8,128)S(1)} %broadcast_in_dim.62, s32[64,256]{1,0:T(8,128)S(1)} %fusion), kind=kLoop, calls=%fused_computation | loop fusion | flops 4712448 | bytes 155648 | tf_op jit(solution)/shard_map/reduce_sum | solution.py:188
  5.2 0.7 %reshape.22.off_ref = s32[6144]{0:T(1024)} reshape(s32[64,96]{1,0:T(8,128)S(1)} %select_reduce_fusion) | data formatting | bytes 49152 | tf_op jit(solution)/shard_map/reshape | solution.py:225
  5.9 1.0 %reduce.1 = s32[2,8192]{1,0:T(2,128)S(1)} reduce(s32[2,8192,1]{1,2,0:T(1,128)} %param.5, s32[]{:T(128)} %constant.39.clone.1), dimensions={2}, to_apply=%param.5.reduce_sub_computation | reduce | bytes 131076 | tf_op args[1]
  6.9 0.1 reshape_reshape.3
  7.1 0.1 fusion.1
  7.2 0.2 fusion.2
  7.4 1.2 %select_reduce_fusion.2 = (s32[32,96]{1,0:T(8,128)S(1)}, s32[32,96]{1,0:T(8,128)S(1)}) fusion(s32[32,256]{1,0:T(8,128)S(1)} %broadcast_add_fusion, s32[32,256]{1,0:T(8,128)S(1)} %fusion.2, s32[32,256]{1,0:T(8,128)S(1)} %fusion.1), kind=kLoop, calls=%fused_computation.6 | loop fusion | flops 4712448 | bytes 122880 | tf_op jit(solution)/shard_map/reduce_sum | solution.py:188
  8.5 0.7 %add_add_fusion.bag_ref = s32[32,192]{1,0:T(8,128)} fusion(s32[32,96]{1,0:T(8,128)S(1)} %get-tuple-element.6, s32[32,96]{1,0:T(8,128)S(1)} %get-tuple-element.5), kind=kLoop, calls=%fused_computation.26 | loop fusion | flops 12288 | bytes 49152 | tf_op jit(solution)/shard_map/sub | solution.py:198
  9.2 56.6 %shard_map.46 = f32[8,128,128]{2,1,0:T(8,128)} custom-call(s32[6144]{0:T(1024)} %reshape.22.off_ref, s32[32,192]{1,0:T(8,128)} %add_add_fusion.bag_ref, f32[2,8192,128]{2,1,0:T(8,128)} %table_hbm.1), custom_call_target="tpu_custom_call" | custom-call | tf_op jit(solution)/shard_map/pallas_call | solution.py:202
  65.9 1.9 %copy.25 = f32[8,128,128]{2,1,0:T(8,128)} copy(f32[8,128,128]{2,1,0:T(8,128)} %shard_map.46) | data formatting | bytes 1048576
  (3 shorter events, 0.0 us)

commit v2 on v1

v2 whole, which is shorter than its diff:
```python
import functools
import jax
import jax.numpy as jnp
from jax import lax
from jax.experimental import pallas as pl
from jax.experimental.pallas import tpu as pltpu
from jax.sharding import PartitionSpec as P

MESH = pl.DeviceIdType.MESH


def kernel(dims, off_ref, bag_ref, table, out_ref, ysend, comb, part, fromleft, fromright,
           ys_sem, yr_sem, zs_sem, lr_sem, rr_sem, fs_sem, fr_sem, own_sem):
    tables, groups, shards, cap, bags = dims
    line = shards // 2
    chips = groups // 2
    pieces = line * groups
    ahead = min(4, pieces)
    g = lax.axis_index("grp")
    r = lax.axis_index("row")
    q = r // 2
    p = r % 2
    mate = q * 2 + 1 - p

    barrier = pltpu.get_barrier_semaphore()
    pl.semaphore_signal(barrier, inc=1, device_id=(g, mate), device_id_type=MESH)

    @pl.when(q > 0)
    def _():
        pl.semaphore_signal(barrier, inc=1, device_id=(g, r - 2), device_id_type=MESH)

    @pl.when(q < line - 1)
    def _():
        pl.semaphore_signal(barrier, inc=1, device_id=(g, r + 2), device_id_type=MESH)

    for step in range(1, groups):
        pl.semaphore_signal(barrier, inc=1, device_id=((g + step) % groups, r), device_id_type=MESH)
    pl.semaphore_wait(barrier, groups + jnp.where(q > 0, 1, 0) + jnp.where(q < line - 1, 1, 0))

    def target(j):
        picked = 0
        for at in range(line):
            order = sorted(range(line), key=lambda d: (-abs(d - at), d))
            for i in range(line):
                picked = picked + jnp.where(jnp.logical_and(q == at, j == i), order[i], 0)
        return picked

    def peer(s):
        return (g // 2 + s // 2) % chips * 2 + (g % 2 + s % 2) % 2

    def origin(s):
        return (g // 2 + chips - s // 2) % chips * 2 + (g % 2 + s % 2) % 2

    def place(n):
        to = target(n // groups)
        s = groups - 1 - n % groups
        return to, s, peer(s)

    def ycopy(c, k):
        return pltpu.make_async_remote_copy(
            src_ref=ysend.at[c, k], dst_ref=comb.at[c, k, 1], send_sem=ys_sem.at[c, k], recv_sem=yr_sem.at[c, k],
            device_id=(g, mate), device_id_type=MESH)

    def rightcopy(c, k):
        return pltpu.make_async_remote_copy(
            src_ref=part.at[c, k], dst_ref=fromleft.at[c, k], send_sem=zs_sem.at[c, k], recv_sem=lr_sem.at[c, k],
            device_id=(g, r + 2), device_id_type=MESH)

    def leftcopy(c, k):
        return pltpu.make_async_remote_copy(
            src_ref=part.at[c, k], dst_ref=fromright.at[c, k], send_sem=zs_sem.at[c, k], recv_sem=rr_sem.at[c, k],
            device_id=(g, r - 2), device_id_type=MESH)

    def ownercopy(c, t, s, k, home):
        return pltpu.make_async_remote_copy(
            src_ref=part.at[c, k], dst_ref=out_ref.at[home * tables + t], send_sem=fs_sem.at[t, s],
            recv_sem=fr_sem.at[t, s], device_id=(k, r), device_id_type=MESH)

    def homecopy(c, t):
        return pltpu.make_async_copy(part.at[c, g], out_ref.at[g * tables + t], own_sem.at[t])

    def gather(t, dst, base):
        @pl.loop(0, cap // 8)
        def _(i):
            for u in range(8):
                row = off_ref[base + i * 8 + u]
                dst[pl.ds(i * 8 + u, 1), :] = table[t, pl.ds(row, 1), :]

    def fetch(n):
        to, s, k = place(n)
        for t in range(tables):
            c = to * tables + t
            first = ((t * groups + k) * line + to) * 2
            gather(t, ysend.at[c, k], (first + 1 - p) * cap)
            ycopy(c, k).start()
        for t in range(tables):
            c = to * tables + t
            first = ((t * groups + k) * line + to) * 2
            gather(t, comb.at[c, k, 0], (first + p) * cap)

    def merge(n):
        to, s, k = place(n)
        places = lax.broadcasted_iota(jnp.int32, (bags, 2 * cap), 0)
        for t in range(tables):
            c = to * tables + t
            spot = (t * groups + k) * line + to
            ycopy(c, k).wait_recv()
            weights = jnp.where(places == bag_ref[pl.ds(spot, 1), :], 1.0, 0.0).astype(jnp.bfloat16)
            vectors = jnp.concatenate([comb[c, k, 0], comb[c, k, 1]], axis=0)
            high = vectors.astype(jnp.bfloat16)
            low = (vectors - high.astype(jnp.float32)).astype(jnp.bfloat16)
            part[c, k] = (jnp.dot(weights, high, preferred_element_type=jnp.float32)
                          + jnp.dot(weights, low, preferred_element_type=jnp.float32))

            @pl.when(jnp.logical_and(to >= q, q > 0))
            def _():
                rightcopy(c, k).wait_recv()
                part[c, k] = part[c, k] + fromleft[c, k]

            @pl.when(jnp.logical_and(to <= q, q < line - 1))
            def _():
                leftcopy(c, k).wait_recv()
                part[c, k] = part[c, k] + fromright[c, k]

            @pl.when(to > q)
            def _():
                rightcopy(c, k).start()

            @pl.when(to < q)
            def _():
                leftcopy(c, k).start()

            @pl.when(jnp.logical_and(to == q, s > 0))
            def _():
                ownercopy(c, t, s, k, g).start()

            @pl.when(jnp.logical_and(to == q, s == 0))
            def _():
                homecopy(c, t).start()

    @pl.loop(0, ahead)
    def _(n):
        fetch(n)

    @pl.loop(0, pieces - ahead)
    def _(n):
        fetch(n + ahead)
        merge(n)

    @pl.loop(pieces - ahead, pieces)
    def _(n):
        merge(n)

    @pl.loop(0, pieces)
    def _(n):
        to, s, k = place(n)
        for t in range(tables):
            c = to * tables + t
            ycopy(c, k).wait_send()

            @pl.when(to != q)
            def _():
                rightcopy(c, k).wait_send()

    @pl.loop(1, groups)
    def _(s):
        for t in range(tables):
            c = q * tables + t
            ownercopy(c, t, s, peer(s), g).wait_send()
            ownercopy(c, t, s, origin(s), origin(s)).wait_recv()

    for t in range(tables):
        homecopy(q * tables + t, t).wait()


def body(table, row_shard, row_offset, bag_lengths):
    groups = lax.axis_size("grp")
    shards = lax.axis_size("row")
    line = shards // 2
    mine = lax.axis_index("row")
    side = mine % 2
    tables, rows, width = table.shape
    bags = bag_lengths.shape[2]
    look = row_offset.shape[1] // (groups * shards)
    cap = 3 * look // shards
    blocks = groups * shards
    owner = row_shard.reshape(tables * blocks, look)
    offset = row_offset.reshape(tables * blocks, look)
    before = jnp.triu(jnp.ones((look, look), jnp.bfloat16), 1)

    def ranks(owners, shard):
        local = owners == shard
        rank = jnp.dot(local.astype(jnp.bfloat16), before, preferred_element_type=jnp.float32).astype(jnp.int32)
        return jnp.where(local, rank, -1)

    def pack(rank, values):
        slots = lax.broadcasted_iota(jnp.int32, (1, cap, 1), 1)
        return jnp.sum(jnp.where(rank[:, None, :] == slots, values[:, None, :], 0), axis=2)

    packed_offset = pack(ranks(owner, mine), offset)
    near = lax.dynamic_index_in_dim(owner.reshape(tables * groups * line, 2, look), side, 1, keepdims=False)
    lengths = lax.dynamic_index_in_dim(bag_lengths.reshape(tables * groups * line, 2, bags), side, 1, keepdims=False)
    upto = jnp.triu(jnp.ones((bags, bags), jnp.bfloat16))
    ends = jnp.dot(lengths.astype(jnp.bfloat16), upto, preferred_element_type=jnp.float32).astype(jnp.int32)
    places = lax.broadcasted_iota(jnp.int32, (1, 1, look), 2)
    within = jnp.sum((ends[:, :, None] <= places).astype(jnp.int32), axis=1)
    mate = mine + 1 - 2 * side
    packed_bag = jnp.concatenate([pack(ranks(near, mine), within + 1), pack(ranks(near, mate), within + 1)], axis=1) - 1

    chunks = line * tables
    dims = (tables, groups, shards, cap, bags)
    return pl.pallas_call(
        functools.partial(kernel, dims),
        out_shape=jax.ShapeDtypeStruct((groups * tables, bags, width), jnp.float32),
        in_specs=[pl.BlockSpec(memory_space=pltpu.SMEM), pl.BlockSpec(memory_space=pltpu.VMEM), pl.BlockSpec(memory_space=pltpu.VMEM)],
        out_specs=pl.BlockSpec(memory_space=pltpu.VMEM),
        scratch_shapes=[
            pltpu.VMEM((chunks, groups, cap, width), jnp.float32),
            pltpu.VMEM((chunks, groups, 2, cap, width), jnp.float32),
            pltpu.VMEM((chunks, groups, bags, width), jnp.float32),
            pltpu.VMEM((chunks, groups, bags, width), jnp.float32),
            pltpu.VMEM((chunks, groups, bags, width), jnp.float32),
            *[pltpu.SemaphoreType.DMA((chunks, groups)) for _ in range(5)],
            pltpu.SemaphoreType.DMA((tables, groups)),
            pltpu.SemaphoreType.DMA((tables, groups)),
            pltpu.SemaphoreType.DMA((tables,)),
        ],
        compiler_params=pltpu.CompilerParams(collective_id=0, has_side_effects=True, vmem_limit_bytes=63 * 2**20),
    )(packed_offset.reshape(-1), packed_bag, table)


def solution(mesh):
    placed = (P("grp", "row", None), P("grp", None, None), P("grp", None), P("grp", None, None))
    return jax.shard_map(
        body, mesh=mesh, in_specs=placed, out_specs=P(None, ("grp", "row"), None), check_vma=False
    )
```

time: 68.2 us -> 60.7 us (0.89)
  the two profiles are of different devices: /device:TPU:17 before, /device:TPU:24 now
where the time goes in v2:
time: 60.7 us; the launch traced here: 60.4 us
  Pallas kernels  49.3 us (81%)
  other arithmetic  6.75 us (11%)
  local copies, waits for them, and re-layouts  3.62 us (6%)
  matrix products  0.66 us (1%)
    pallas_call x1, Pallas kernels, body(): pl.pallas_call(functools.partial(kernel, dims), out_shape=jax.ShapeDtypeS...  49.3 us
    reduce_sum x2, other arithmetic, pack(): jnp.sum(jnp.where(rank[:, None, :] == slots, values[:, None, :], 0), axis=2)  2.47 us
    unnamed x1, local copies, waits for them, and re-layouts  1.87 us

profile of v2, /device:TPU:24, one launch (start us, length us, event | category | flops | bytes accessed | tf_op | source)
XLA Modules:
  0.0 60.4 jit_solution(240471352306855452)
XLA Ops:
  0.0 0.8 %dynamic-slice_convert_fusion = bf16[32,1,128]{2,1,0:T(2,128)(2,1)S(1)} fusion(s32[32,2,128]{2,1,0:T(2,128)} %bitcast.11, s32[]{:T(128)S(6)} %select_n.51), kind=kLoop, calls=%fused_computation.38 | loop fusion | flops 4096 | bytes 24580 | tf_op jit(solution)/shard_map/convert_element_type | solution.py:204
  0.8 0.2 convolution_convert_fusion.3
  1.0 0.7 %convert_reduce_fusion = s32[32,256]{1,0:T(8,128)S(1)} fusion(s32[32,128]{1,0:T(8,128)S(1)} %convolution_convert_fusion.3), kind=kLoop, calls=%fused_computation.2 | loop fusion | flops 3137536 | bytes 49152 | tf_op jit(solution)/shard_map/reduce_sum | solution.py:206
  1.7 1.1 %compare_reduce_fusion = pred[2,8192]{1,0:T(4,128)(4,1)S(1)} fusion(s32[2,8192,1]{1,2,0:T(1,128)} %param.5, s32[]{:T(128)S(6)} %axis_index.12), kind=kLoop, calls=%fused_computation.17 | loop fusion | flops 16384 | bytes 81924 | tf_op jit(solution)/shard_map/eq | solution.py:192
  2.8 0.1 eq.70
  2.8 0.2 fusion
  3.0 0.9 %broadcast_in_dim.62 = s32[64,256]{1,0:T(8,128)S(1)} reshape(s32[2,8192]{1,0:T(2,128)} %param.6) | data formatting | bytes 131072 | tf_op jit(solution)/shard_map/jit(_where)/broadcast_in_dim | solution.py:198
  3.9 1.3 %select_reduce_fusion = s32[64,96]{1,0:T(8,128)S(1)} fusion(s32[64,256]{1,0:T(8,128)S(1)} %broadcast_in_dim.62, s32[64,256]{1,0:T(8,128)S(1)} %fusion), kind=kLoop, calls=%fused_computation | loop fusion | flops 4712448 | bytes 155648 | tf_op jit(solution)/shard_map/reduce_sum | solution.py:198
  5.2 0.7 %reshape.22.off_ref = s32[6144]{0:T(1024)} reshape(s32[64,96]{1,0:T(8,128)S(1)} %select_reduce_fusion) | data formatting | bytes 49152 | tf_op jit(solution)/shard_map/reshape | solution.py:229
  5.9 1.0 %reduce.1 = s32[2,8192]{1,0:T(2,128)S(1)} reduce(s32[2,8192,1]{1,2,0:T(1,128)} %param.5, s32[]{:T(128)} %constant.39.clone.1), dimensions={2}, to_apply=%param.5.reduce_sub_computation | reduce | bytes 131076 | tf_op args[1]
  6.9 0.1 reshape_reshape.3
  7.1 0.1 fusion.1
  7.2 0.2 fusion.2
  7.4 1.2 %select_reduce_fusion.2 = (s32[32,96]{1,0:T(8,128)S(1)}, s32[32,96]{1,0:T(8,128)S(1)}) fusion(s32[32,256]{1,0:T(8,128)S(1)} %broadcast_add_fusion, s32[32,256]{1,0:T(8,128)S(1)} %fusion.2, s32[32,256]{1,0:T(8,128)S(1)} %fusion.1), kind=kLoop, calls=%fused_computation.6 | loop fusion | flops 4712448 | bytes 122880 | tf_op jit(solution)/shard_map/reduce_sum | solution.py:198
  8.5 0.7 %add_add_fusion.bag_ref = s32[32,192]{1,0:T(8,128)} fusion(s32[32,96]{1,0:T(8,128)S(1)} %get-tuple-element.6, s32[32,96]{1,0:T(8,128)S(1)} %get-tuple-element.5), kind=kLoop, calls=%fused_computation.26 | loop fusion | flops 12288 | bytes 49152 | tf_op jit(solution)/shard_map/sub | solution.py:208
  9.2 49.3 %shard_map.46 = f32[8,128,128]{2,1,0:T(8,128)} custom-call(s32[6144]{0:T(1024)} %reshape.22.off_ref, s32[32,192]{1,0:T(8,128)} %add_add_fusion.bag_ref, f32[2,8192,128]{2,1,0:T(8,128)} %table.1), custom_call_target="tpu_custom_call" | custom-call | tf_op jit(solution)/shard_map/pallas_call | solution.py:212
  58.5 1.9 %copy.25 = f32[8,128,128]{2,1,0:T(8,128)} copy(f32[8,128,128]{2,1,0:T(8,128)} %shard_map.46) | data formatting | bytes 1048576
  (3 shorter events, 0.0 us)

commit v3 on v2

v3 whole, which is shorter than its diff:
```python
import functools
import jax
import jax.numpy as jnp
from jax import lax
from jax.experimental import pallas as pl
from jax.experimental.pallas import tpu as pltpu
from jax.sharding import PartitionSpec as P

MESH = pl.DeviceIdType.MESH


def kernel(dims, shard_ref, offset_ref, length_ref, table_hbm, out_ref, *scratch):
    tables, groups, shards, cap, bags, look = dims
    held = scratch[:tables]
    (ysend, comb, part, fromleft, fromright, weights_of, staged, off_ref, earlier, starts_of, ends_of,
     ys_sem, yr_sem, zs_sem, lr_sem, rr_sem, fs_sem, fr_sem, own_sem, tab_sem, off_sem) = scratch[tables:]
    lanes = shard_ref.shape[1]
    halves = look // lanes
    blocks = groups * shards
    slots = weights_of.shape[0]
    line = shards // 2
    chips = groups // 2
    pieces = line * groups
    ahead = weights_of.shape[0] - 3
    g = lax.axis_index("grp")
    r = lax.axis_index("row")
    q = r // 2
    p = r % 2
    mate = q * 2 + 1 - p

    loads = [pltpu.make_async_copy(table_hbm.at[t], held[t], tab_sem.at[t]) for t in range(tables)]
    for load in loads:
        load.start()

    barrier = pltpu.get_barrier_semaphore()
    pl.semaphore_signal(barrier, inc=1, device_id=(g, mate), device_id_type=MESH)

    @pl.when(q > 0)
    def _():
        pl.semaphore_signal(barrier, inc=1, device_id=(g, r - 2), device_id_type=MESH)

    @pl.when(q < line - 1)
    def _():
        pl.semaphore_signal(barrier, inc=1, device_id=(g, r + 2), device_id_type=MESH)

    for step in range(1, groups):
        pl.semaphore_signal(barrier, inc=1, device_id=((g + step) % groups, r), device_id_type=MESH)

    def ones_where(keep):
        return jnp.where(keep, 1.0, 0.0).astype(jnp.bfloat16)

    def grid_of(size):
        return [lax.broadcasted_iota(jnp.int32, (size, size), axis) for axis in range(2)]

    down, across = grid_of(look)
    earlier[...] = ones_where(down < across)
    down, across = grid_of(bags)
    starts_of[...] = ones_where(across < down)
    ends_of[...] = ones_where(across <= down)

    def target(j):
        picked = 0
        for at in range(line):
            order = sorted(range(line), key=lambda d: (-abs(d - at), d))
            for i in range(line):
                picked = picked + jnp.where(jnp.logical_and(q == at, j == i), order[i], 0)
        return picked

    def peer(s):
        return (g // 2 + s // 2) % chips * 2 + (g % 2 + s % 2) % 2

    def origin(s):
        return (g // 2 + chips - s // 2) % chips * 2 + (g % 2 + s % 2) % 2

    def place(n):
        to = target(n // groups)
        s = groups - 1 - n % groups
        return to, s, peer(s)

    def ycopy(c, k):
        return pltpu.make_async_remote_copy(
            src_ref=ysend.at[c, k], dst_ref=comb.at[c, k, 1], send_sem=ys_sem.at[c, k], recv_sem=yr_sem.at[c, k],
            device_id=(g, mate), device_id_type=MESH)

    def rightcopy(c, k):
        return pltpu.make_async_remote_copy(
            src_ref=part.at[c, k], dst_ref=fromleft.at[c, k], send_sem=zs_sem.at[c, k], recv_sem=lr_sem.at[c, k],
            device_id=(g, r + 2), device_id_type=MESH)

    def leftcopy(c, k):
        return pltpu.make_async_remote_copy(
            src_ref=part.at[c, k], dst_ref=fromright.at[c, k], send_sem=zs_sem.at[c, k], recv_sem=rr_sem.at[c, k],
            device_id=(g, r - 2), device_id_type=MESH)

    def ownercopy(c, t, s, k, home):
        return pltpu.make_async_remote_copy(
            src_ref=part.at[c, k], dst_ref=out_ref.at[home * tables + t], send_sem=fs_sem.at[t, s],
            recv_sem=fr_sem.at[t, s], device_id=(k, r), device_id_type=MESH)

    def homecopy(c, t):
        return pltpu.make_async_copy(part.at[c, g], out_ref.at[g * tables + t], own_sem.at[t])

    def across_lanes(a, b):
        return lax.dot_general(a, b, (((1,), (1,)), ((), ())), preferred_element_type=jnp.float32)

    def shards_at(t, o):
        return jnp.concatenate([shard_ref[pl.ds((t * blocks + o) * halves + h, 1), :] for h in range(halves)], axis=1)

    def offsets_at(t, o):
        return jnp.concatenate([offset_ref[pl.ds((o * halves + h) * tables + t, 1), :] for h in range(halves)], axis=1)

    def prepare(n):
        to, s, k = place(n)
        slot = n % slots
        away, here = (k * line + to) * 2 + 1 - p, (k * line + to) * 2 + p
        local = []
        for t in range(tables):
            local.append(jnp.where(shards_at(t, away) == r, 1.0, 0.0))
            local.append(jnp.where(shards_at(t, here) == r, 1.0, 0.0))
            local.append(jnp.where(shards_at(t, here) == mate, 1.0, 0.0))
        local += [jnp.zeros_like(local[0])] * (-len(local) % 8)
        local = jnp.concatenate(local, axis=0)
        rank = jnp.dot(local.astype(jnp.bfloat16), earlier[...], preferred_element_type=jnp.float32)
        rank = jnp.where(local > 0.5, rank, -1.0).astype(jnp.int32)
        slot_ids = lax.broadcasted_iota(jnp.int32, (cap, look), 0)
        places = lax.broadcasted_iota(jnp.int32, (bags, look), 1).astype(jnp.float32)
        for t in range(tables):
            sent, kept, given = [ones_where(rank[3 * t + i:3 * t + i + 1, :] == slot_ids) for i in range(3)]
            for i, (o, chosen) in enumerate(((away, sent), (here, kept))):
                wanted = offsets_at(t, o)
                digits = [wanted // 128, wanted % 128] + [jnp.zeros_like(wanted)] * 6
                digits = jnp.concatenate(digits, axis=0).astype(jnp.float32).astype(jnp.bfloat16)
                packed = across_lanes(digits, chosen)
                index = packed[0:1, :] * 128.0 + packed[1:2, :]
                index = jnp.clip(index.astype(jnp.int32), 0, held[t].shape[0] - 1)
                staged[slot, pl.ds(2 * t + i, 1), pl.ds(0, cap)] = index
            lengths = length_ref[pl.ds(t * blocks + here, 1), :].astype(jnp.float32)
            lengths = jnp.broadcast_to(lengths, (8, bags)).astype(jnp.bfloat16)
            starts = across_lanes(starts_of[...], lengths)[:, 0:1]
            ends = across_lanes(ends_of[...], lengths)[:, 0:1]
            member = ones_where(jnp.logical_and(places >= starts, places < ends))
            weights = across_lanes(member, jnp.concatenate([kept, given], axis=0))
            weights_of[slot, t] = weights.astype(jnp.bfloat16)

    def toscalars(n):
        slot = n % slots
        return pltpu.make_async_copy(staged.at[slot], off_ref.at[slot], off_sem.at[slot])

    def gather(slot, t, i, dst):
        @pl.loop(0, cap // 8)
        def _(b):
            for u in range(8):
                row = off_ref[slot, 2 * t + i, b * 8 + u]
                dst[pl.ds(b * 8 + u, 1), :] = held[t][pl.ds(row, 1), :]

    def fetch(n):
        to, s, k = place(n)
        slot = n % slots
        toscalars(n).wait()
        for t in range(tables):
            c = to * tables + t
            gather(slot, t, 0, ysend.at[c, k])
            ycopy(c, k).start()
        for t in range(tables):
            gather(slot, t, 1, comb.at[to * tables + t, k, 0])

    def merge(n):
        to, s, k = place(n)
        for t in range(tables):
            c = to * tables + t
            ycopy(c, k).wait_recv()
            weights = weights_of[n % slots, t]
            vectors = jnp.concatenate([comb[c, k, 0], comb[c, k, 1]], axis=0)
            high = vectors.astype(jnp.bfloat16)
            low = (vectors - high.astype(jnp.float32)).astype(jnp.bfloat16)
            part[c, k] = (jnp.dot(weights, high, preferred_element_type=jnp.float32)
                          + jnp.dot(weights, low, preferred_element_type=jnp.float32))

            @pl.when(jnp.logical_and(to >= q, q > 0))
            def _():
                rightcopy(c, k).wait_recv()
                part[c, k] = part[c, k] + fromleft[c, k]

            @pl.when(jnp.logical_and(to <= q, q < line - 1))
            def _():
                leftcopy(c, k).wait_recv()
                part[c, k] = part[c, k] + fromright[c, k]

            @pl.when(to > q)
            def _():
                rightcopy(c, k).start()

            @pl.when(to < q)
            def _():
                leftcopy(c, k).start()

            @pl.when(jnp.logical_and(to == q, s > 0))
            def _():
                ownercopy(c, t, s, k, g).start()

            @pl.when(jnp.logical_and(to == q, s == 0))
            def _():
                homecopy(c, t).start()

    prepare(0)
    prepare(1)
    toscalars(0).start()
    for load in loads:
        load.wait()
    pl.semaphore_wait(barrier, groups + jnp.where(q > 0, 1, 0) + jnp.where(q < line - 1, 1, 0))

    @pl.loop(2, pieces + ahead + 2)
    def _(m):
        @pl.when(m - 2 < pieces)
        def _():
            fetch(m - 2)

        @pl.when(m - 1 < pieces)
        def _():
            toscalars(m - 1).start()

        @pl.when(m < pieces)
        def _():
            prepare(m)

        @pl.when(m - 2 - ahead >= 0)
        def _():
            merge(m - 2 - ahead)

    @pl.loop(0, pieces)
    def _(n):
        to, s, k = place(n)
        for t in range(tables):
            c = to * tables + t
            ycopy(c, k).wait_send()

            @pl.when(to != q)
            def _():
                rightcopy(c, k).wait_send()

    @pl.loop(1, groups)
    def _(s):
        for t in range(tables):
            c = q * tables + t
            ownercopy(c, t, s, peer(s), g).wait_send()
            ownercopy(c, t, s, origin(s), origin(s)).wait_recv()

    for t in range(tables):
        homecopy(q * tables + t, t).wait()


def body(table, row_shard, row_offset, bag_lengths):
    groups = lax.axis_size("grp")
    shards = lax.axis_size("row")
    line = shards // 2
    tables, rows, width = table.shape
    bags = bag_lengths.shape[2]
    blocks = groups * shards
    look = row_offset.shape[1] // blocks
    cap = 3 * look // shards
    lanes = min(look, 128)
    strips = row_offset.shape[1] // lanes
    chunks = line * tables
    slots = 7
    held_rows = -(-2 * tables // 8) * 8
    dims = (tables, groups, shards, cap, bags, look)
    vector, dma = pltpu.VMEM, pltpu.SemaphoreType.DMA
    in_vmem = pl.BlockSpec(memory_space=pltpu.VMEM)
    return pl.pallas_call(
        functools.partial(kernel, dims),
        out_shape=jax.ShapeDtypeStruct((groups * tables, bags, width), jnp.float32),
        in_specs=[in_vmem, in_vmem, in_vmem, pl.BlockSpec(memory_space=pl.ANY)],
        out_specs=in_vmem,
        scratch_shapes=[
            *[vector((rows, width), jnp.float32) for _ in range(tables)],
            vector((chunks, groups, cap, width), jnp.float32),
            vector((chunks, groups, 2, cap, width), jnp.float32),
            *[vector((chunks, groups, bags, width), jnp.float32) for _ in range(3)],
            vector((slots, tables, bags, 2 * cap), jnp.bfloat16),
            vector((slots, held_rows, 128), jnp.int32),
            pltpu.SMEM((slots, held_rows, 128), jnp.int32),
            vector((look, look), jnp.bfloat16),
            vector((bags, bags), jnp.bfloat16),
            vector((bags, bags), jnp.bfloat16),
            *[dma((chunks, groups)) for _ in range(5)],
            dma((tables, groups)),
            dma((tables, groups)),
            dma((tables,)),
            dma((tables,)),
            dma((slots,)),
        ],
        compiler_params=pltpu.CompilerParams(collective_id=0, has_side_effects=True, vmem_limit_bytes=63 * 2**20),
    )(
        row_shard.reshape(tables * strips, lanes),
        row_offset.reshape(tables, strips, lanes).swapaxes(0, 1).reshape(strips * tables, lanes),
        bag_lengths.reshape(tables * blocks, bags),
        table,
    )


def solution(mesh):
    placed = (P("grp", "row", None), P("grp", None, None), P("grp", None), P("grp", None, None))
    return jax.shard_map(
        body, mesh=mesh, in_specs=placed, out_specs=P(None, ("grp", "row"), None), check_vma=False
    )
```

time: 60.7 us -> 58.9 us (0.970); the launches traced: 60.4 us -> 58 us
  Pallas kernels: 49.3 us -> 56.1 us
  other arithmetic: 6.75 us -> 0 us
  local copies, waits for them, and re-layouts: 3.62 us -> 1.87 us
  matrix products: 0.66 us -> 0 us
    pallas_call x1, Pallas kernels: 49.3 us -> 56.1 us  [body(): pl.pallas_call(functools.partial(kernel, dims), out_shape=jax.ShapeDtypeS...]
    reduce_sum x3 -> x0, other arithmetic: 3.18 us -> none  [the longest x2 2.47 us: pack(): jnp.sum(jnp.where(rank[:, None, :] == slots, values[:, None, :], 0), axis=2)]
    eq x1 -> x0, other arithmetic: 1.06 us -> none  [ranks(): local = owners == shard]
    unnamed x1 -> x0, other arithmetic: 1.03 us -> none
    broadcast_in_dim x1 -> x0, local copies, waits for them, and re-layouts: 0.9 us -> none  [pack(): jnp.where(rank[:, None, :] == slots, values[:, None, :], 0)]
    convert_element_type x1 -> x0, other arithmetic: 0.78 us -> none  [body(): lengths.astype(jnp.bfloat16)]
    sub x1 -> x0, other arithmetic: 0.7 us -> none  [body(): jnp.concatenate([pack(ranks(near, mine), within + 1), pack(ranks(near, ma...]
    reshape x1 -> x0, local copies, waits for them, and re-layouts: 0.68 us -> none  [body(): packed_offset.reshape(-1)]
where the time goes in v3:
time: 58.9 us; the launch traced here: 58 us
  Pallas kernels  56.1 us (95%)
  local copies, waits for them, and re-layouts  1.87 us (3%)
    pallas_call x1, Pallas kernels, body(): pl.pallas_call(functools.partial(kernel, dims), out_shape=jax.ShapeDtypeS...  56.1 us
    unnamed x1, local copies, waits for them, and re-layouts  1.87 us

profile of v3, /device:TPU:24, one launch (start us, length us, event | category | flops | bytes accessed | tf_op | source)
XLA Modules:
  0.0 58.0 jit_solution(17060186036189646373)
XLA Ops:
  0.0 56.1 %shard_map.46 = f32[8,128,128]{2,1,0:T(8,128)} custom-call(s32[128,128]{1,0:T(8,128)} %bitcast.7, s32[128,128]{1,0:T(8,128)} %bitcast.8, s32[64,128]{1,0:T(8,128)} %bitcast.9, f32[2,8192,128]{2,1,0:T(8,128)} %table_hbm.1), custom_call_target="tpu_custom_call" | custom-call | tf_op jit(solution)/shard_map/pallas_call | solution.py:269
  56.1 1.9 %copy.7 = f32[8,128,128]{2,1,0:T(8,128)} copy(f32[8,128,128]{2,1,0:T(8,128)} %shard_map.46) | data formatting | bytes 1048576

commit v4 on v3

--- a/solution.py
+++ b/solution.py
@@ -153,12 +153,14 @@
                 row = off_ref[slot, 2 * t + i, b * 8 + u]
                 dst[pl.ds(b * 8 + u, 1), :] = held[t][pl.ds(row, 1), :]
 
-    def fetch(n):
+    def fetch(n, first=False):
         to, s, k = place(n)
         slot = n % slots
         toscalars(n).wait()
         for t in range(tables):
             c = to * tables + t
+            if first:
+                loads[t].wait()
             gather(slot, t, 0, ysend.at[c, k])
             ycopy(c, k).start()
         for t in range(tables):
@@ -166,6 +168,7 @@
 
     def merge(n):
         to, s, k = place(n)
+        sums = []
         for t in range(tables):
             c = to * tables + t
             ycopy(c, k).wait_recv()
@@ -173,8 +176,13 @@
             vectors = jnp.concatenate([comb[c, k, 0], comb[c, k, 1]], axis=0)
             high = vectors.astype(jnp.bfloat16)
             low = (vectors - high.astype(jnp.float32)).astype(jnp.bfloat16)
-            part[c, k] = (jnp.dot(weights, high, preferred_element_type=jnp.float32)
-                          + jnp.dot(weights, low, preferred_element_type=jnp.float32))
+            sums.append(jnp.dot(weights, high, preferred_element_type=jnp.float32)
+                        + jnp.dot(weights, low, preferred_element_type=jnp.float32))
+        for t in range(tables):
+            c = to * tables + t
+            part[c, k] = sums[t]
+        for t in range(tables):
+            c = to * tables + t
 
             @pl.when(jnp.logical_and(to >= q, q > 0))
             def _():
@@ -205,11 +213,13 @@
     prepare(0)
     prepare(1)
     toscalars(0).start()
-    for load in loads:
-        load.wait()
     pl.semaphore_wait(barrier, groups + jnp.where(q > 0, 1, 0) + jnp.where(q < line - 1, 1, 0))
 
-    @pl.loop(2, pieces + ahead + 2)
+    fetch(0, True)
+    toscalars(1).start()
+    prepare(2)
+
+    @pl.loop(3, pieces + ahead + 2)
     def _(m):
         @pl.when(m - 2 < pieces)
         def _():
@@ -219,13 +229,13 @@
         def _():
             toscalars(m - 1).start()
 
+        @pl.when(m - 2 - ahead >= 0)
+        def _():
+            merge(m - 2 - ahead)
+
         @pl.when(m < pieces)
         def _():
             prepare(m)
-
-        @pl.when(m - 2 - ahead >= 0)
-        def _():
-            merge(m - 2 - ahead)
 
     @pl.loop(0, pieces)
     def _(n):
@@ -261,7 +271,7 @@
     lanes = min(look, 128)
     strips = row_offset.shape[1] // lanes
     chunks = line * tables
-    slots = 7
+    slots = 5
     held_rows = -(-2 * tables // 8) * 8
     dims = (tables, groups, shards, cap, bags, look)
     vector, dma = pltpu.VMEM, pltpu.SemaphoreType.DMA

time: 58.9 us -> 58 us (0.985)
  the two profiles are of different devices: /device:TPU:24 before, /device:TPU:16 now
where the time goes in v4:
time: 58 us; the launch traced here: 57.8 us
  Pallas kernels  55.9 us (96%)
  local copies, waits for them, and re-layouts  1.87 us (3%)
    pallas_call x1, Pallas kernels, body(): pl.pallas_call(functools.partial(kernel, dims), out_shape=jax.ShapeDtypeS...  55.9 us
    unnamed x1, local copies, waits for them, and re-layouts  1.87 us

profile of v4, /device:TPU:16, one launch (start us, length us, event | category | flops | bytes accessed | tf_op | source)
XLA Modules:
  0.0 57.8 jit_solution(7956387775195493222)
XLA Ops:
  0.0 55.9 %shard_map.46 = f32[8,128,128]{2,1,0:T(8,128)} custom-call(s32[128,128]{1,0:T(8,128)} %bitcast.7, s32[128,128]{1,0:T(8,128)} %bitcast.8, s32[64,128]{1,0:T(8,128)} %bitcast.9, f32[2,8192,128]{2,1,0:T(8,128)} %table_hbm.1), custom_call_target="tpu_custom_call" | custom-call | tf_op jit(solution)/shard_map/pallas_call | solution.py:279
  56.0 1.9 %copy.7 = f32[8,128,128]{2,1,0:T(8,128)} copy(f32[8,128,128]{2,1,0:T(8,128)} %shard_map.46) | data formatting | bytes 1048576

commit v5 on v4

--- a/solution.py
+++ b/solution.py
@@ -215,27 +215,36 @@
     toscalars(0).start()
     pl.semaphore_wait(barrier, groups + jnp.where(q > 0, 1, 0) + jnp.where(q < line - 1, 1, 0))
 
-    fetch(0, True)
-    toscalars(1).start()
-    prepare(2)
-
-    @pl.loop(3, pieces + ahead + 2)
-    def _(m):
-        @pl.when(m - 2 < pieces)
+    def advance(m, first=False):
+        fetch(m, first)
+
+        @pl.when(m + 1 < pieces)
         def _():
-            fetch(m - 2)
-
-        @pl.when(m - 1 < pieces)
+            toscalars(m + 1).start()
+
+        @pl.when(m + 2 < pieces)
         def _():
-            toscalars(m - 1).start()
-
-        @pl.when(m - 2 - ahead >= 0)
-        def _():
-            merge(m - 2 - ahead)
-
-        @pl.when(m < pieces)
-        def _():
-            prepare(m)
+            prepare(m + 2)
+
+    advance(0, True)
+    advance(1)
+    merge(0)
+
+    @pl.loop(1, ahead)
+    def _(n):
+        @pl.loop(0, 2)
+        def _(u):
+            advance(2 * n + u)
+        merge(n)
+
+    @pl.loop(ahead, pieces - ahead)
+    def _(n):
+        advance(n + ahead)
+        merge(n)
+
+    @pl.loop(pieces - ahead, pieces)
+    def _(n):
+        merge(n)
 
     @pl.loop(0, pieces)
     def _(n):
@@ -271,7 +280,7 @@
     lanes = min(look, 128)
     strips = row_offset.shape[1] // lanes
     chunks = line * tables
-    slots = 5
+    slots = min(6, line * groups // 2) + 3
     held_rows = -(-2 * tables // 8) * 8
     dims = (tables, groups, shards, cap, bags, look)
     vector, dma = pltpu.VMEM, pltpu.SemaphoreType.DMA

time: 58 us -> 58.9 us (1.016)
  the two profiles are of different devices: /device:TPU:16 before, /device:TPU:24 now
where the time goes in v5:
time: 58.9 us; the launch traced here: 58.6 us
  Pallas kernels  56.7 us (96%)
  local copies, waits for them, and re-layouts  1.87 us (3%)
    pallas_call x1, Pallas kernels, body(): pl.pallas_call(functools.partial(kernel, dims), out_shape=jax.ShapeDtypeS...  56.7 us
    unnamed x1, local copies, waits for them, and re-layouts  1.87 us

profile of v5, /device:TPU:24, one launch (start us, length us, event | category | flops | bytes accessed | tf_op | source)
XLA Modules:
  0.0 58.6 jit_solution(6237093055141823342)
XLA Ops:
  0.0 56.7 %shard_map.46 = f32[8,128,128]{2,1,0:T(8,128)} custom-call(s32[128,128]{1,0:T(8,128)} %bitcast.7, s32[128,128]{1,0:T(8,128)} %bitcast.8, s32[64,128]{1,0:T(8,128)} %bitcast.9, f32[2,8192,128]{2,1,0:T(8,128)} %table_hbm.1), custom_call_target="tpu_custom_call" | custom-call | tf_op jit(solution)/shard_map/pallas_call | solution.py:288
  56.7 1.9 %copy.7 = f32[8,128,128]{2,1,0:T(8,128)} copy(f32[8,128,128]{2,1,0:T(8,128)} %shard_map.46) | data formatting | bytes 1048576
